TPU v7x, 32 devices: a whole 2x2x4 slice. The times are simulated.
32 devices in a mesh: prow: 4 (over z), pcol: 8 (over y, x, core).
Axes of the slice: x: 2, y: 2, z: 4, core: 2. Of those that a mesh axis runs over, the one named last changes fastest.
Arguments:
- ainv_in: float32 [36, 4, 18, 8, 128, 128], P(None, 'prow', None, 'pcol'), as said below
- ufactor: bfloat16 [36, 4, 6, 128, 128], P(None, 'prow'), may hold values from -0.08984375 to 0.08984375
- dinv: float32 [6, 128, 128], replicated, may hold values from -6 to 6
- pattern: int32 [144, 144], replicated, may hold values from 0 to 1, as said below
Outputs:
- ainv_out: float32 [36, 4, 18, 8, 128, 128], P(None, 'prow', None, 'pcol')
Inputs may be any that keep to these rules, and one draw needn't show every extreme that they name: For a column j below 6, pattern[i, j] is 0 for i <= j, 1 at the parent row (the nearest row below j that has a 1, at most 3 below j), and the other 1s of column j lie in rows where the parent's column has a 1; for j at least 6, pattern[i, j] is 1 exactly where i > j. `ainv_in`: a symmetric matrix.
All inputs are finite; a program needn't handle non-finite values.
Results may differ from a plain program's by a relative error of at most 0.0003.
Values may be sent and summed in bfloat16 or wider, within the bound.
A program may use at most 192 MiB of HBM per device.

v0:
```python
import jax
import jax.numpy as jnp
from jax import lax
from jax.sharding import PartitionSpec as P


def spread(value, axis, source):
    kept = jnp.where(lax.axis_index(axis) == source, value, 0).astype(value.dtype)
    return lax.psum(kept, axis)


def per_device(ainv_in, ufactor, dinv, pattern):
    row_blocks, _, col_blocks, _, width, _ = ainv_in.shape
    step_count = dinv.shape[0]
    blocks = ainv_in.reshape(row_blocks, col_blocks, width, width)
    lower = ufactor.reshape(row_blocks, step_count, width, width)
    row_count = lax.axis_size("prow")
    col_count = lax.axis_size("pcol")
    prow_id = lax.axis_index("prow")
    pcol_id = lax.axis_index("pcol")
    row_ids = jnp.arange(row_blocks, dtype=jnp.int32) * row_count + prow_id
    col_ids = jnp.arange(col_blocks, dtype=jnp.int32) * col_count + pcol_id
    fold_ratio = col_count // row_count
    pick_slot = pcol_id // row_count
    home_row = pcol_id % row_count
    mask_rows = pattern[row_ids, :]
    live_lower = mask_rows[:, :step_count] > 0
    masked_lower = jnp.where(live_lower[:, :, None, None], lower, jnp.zeros_like(lower))
    chosen_cols = lax.dynamic_index_in_dim(
        masked_lower.reshape(col_blocks, fold_ratio, step_count, width, width),
        pick_slot,
        1,
        keepdims=False,
    )
    other_cols = spread(chosen_cols, "prow", home_row)

    def fetch(column):
        own_col = lax.dynamic_index_in_dim(masked_lower, column, 1, keepdims=False)
        other_rows = lax.dynamic_index_in_dim(other_cols, column, 1, keepdims=False)
        return (own_col, other_rows)

    def advance(taken, matrix):
        column = step_count - 1 - taken
        own_col, other_rows = fetch(column)
        partial_value = -jnp.einsum(
            "acxy,cyz->axz", matrix, other_rows.astype(jnp.float32), precision=lax.Precision.HIGHEST
        )
        col_piece = lax.psum_scatter(partial_value, "pcol", scatter_dimension=1, tiled=True)
        col_whole = lax.all_gather(col_piece, "pcol", axis=1, tiled=True)
        live_rows = lax.dynamic_index_in_dim(mask_rows, column, 1, keepdims=False) > 0
        inverse_col = jnp.where(live_rows[:, None, None], col_whole, jnp.zeros_like(col_whole))
        diag_term = jnp.einsum(
            "axy,axz->yz", own_col.astype(jnp.float32), inverse_col, precision=lax.Precision.HIGHEST
        )
        diag_total = lax.psum(diag_term, "prow")
        diag_block = lax.dynamic_index_in_dim(dinv, column, 0, keepdims=False) - diag_total
        new_col = jnp.where((row_ids == column)[:, None, None], diag_block[None], inverse_col)
        col_slot = column // col_count
        old_col = lax.dynamic_index_in_dim(matrix, col_slot, 1, keepdims=False)
        matrix = lax.dynamic_update_index_in_dim(
            matrix, jnp.where(pcol_id == column % col_count, new_col, old_col), col_slot, 1
        )
        chosen = lax.dynamic_index_in_dim(
            inverse_col.reshape(col_blocks, fold_ratio, width, width), pick_slot, 1, keepdims=False
        )
        across = spread(chosen, "prow", home_row)
        row_vals = jnp.where((col_ids == column)[:, None, None], diag_block[None], across)
        row_vals = jnp.swapaxes(row_vals, 1, 2)
        row_slot = column // row_count
        old_row = lax.dynamic_index_in_dim(matrix, row_slot, 0, keepdims=False)
        matrix = lax.dynamic_update_index_in_dim(
            matrix, jnp.where(prow_id == column % row_count, row_vals, old_row), row_slot, 0
        )
        return matrix

    blocks = lax.fori_loop(0, step_count, advance, blocks)
    return blocks.reshape(ainv_in.shape)


def solution(mesh):
    placed = (
        P(None, "prow", None, "pcol", None, None),
        P(None, "prow", None, None, None),
        P(),
        P(),
    )
    return jax.shard_map(
        per_device,
        mesh=mesh,
        in_specs=placed,
        out_specs=P(None, "prow", None, "pcol", None, None),
        check_vma=False,
    )
```

profile of v0, /device:TPU:0, one launch (start us, length us, event | category | flops | bytes accessed | tf_op | source)
XLA Modules:
  0.0 1241.6 jit_solution(2986418367816600455)
XLA Ops:
  6.5 30.5 %copy.57 = f32[36,1,18,1,128,128]{5,4,3,2,1,0:T(8,128)} copy(f32[36,1,18,1,128,128]{5,4,3,2,1,0:T(8,128)} %param.6) | data formatting | bytes 84934656
  37.8 4.3 fusion.16
  42.2 10.4 copy.31
  52.7 6.5 bitcast_select_fusion.2
  59.1 119.6 %all-reduce.6.cloned.1.call-done = bf16[18,6,128,128]{3,2,1,0:T(8,128)(2,1)} async-done(((bf16[18,6,128,128]{3,2,1,0:T(8,128)(2,1)}), bf16[18,6,128,128]{3,2,1,0:T(8,128)(2,1)}) %all-reduce.6.cloned.1.call-update) | async-done | bytes 3538960 | tf_op jit(solution)/shard_map/psum | solution.py:9
  178.7 1055.4 %while.18 = (s32[]{:T(128)}, f32[36,18,128,128]{3,2,1,0:T(8,128)}, s32[]{:T(128)}, f32[6,128,128]{2,1,0:T(8,128)}, bf16[36,6,128,128]{2,3,0,1:T(8,128)(2,1)}, /*...) while((s32[]{:T(128)}, f32[36,18,128,128]{3,2,1,0:T(8,128)}, ...), condition=%wide.region_5.6_spmd.clone.clone, body=%wide.region_1.5_spmd.clone.clone.sunk | while | flops 17217585152 | bytes 122127656 | solution.py:76
  178.7 27.0 %fusion.30 = f32[36,128,128]{1,2,0:T(8,128)S(1)} fusion(f32[36,18,128,128]{3,2,1,0:T(8,128)} %get-tuple-element.557, bf16[18,6,128,128]{3,2,1,0:T(8,128)(2,1)} %get-tuple-element.586, s32[]{:T(128)S(6)} %select_n.384), kind=kOutput, calls=%fused_computation.6.clone.1 | convolution fusion | flops 16308043776 | bytes 45416452 | tf_op jit(solution)/shard_map/while/body/eval_jaxpr/acxy,cyz->axz/dot_general | solution.py:45
  205.8 2.3 copy.41
  208.1 42.6 %reduce-scatter.2.cloned.1.call-done = f32[36,16,128]{2,0,1:T(8,128)} async-done(((f32[36,128,128]{2,0,1:T(8,128)}), f32[36,16,128]{2,0,1:T(8,128)}) %reduce-scatter.2.cloned.1.call-update) | async-done | bytes 294928 | tf_op jit(solution)/shard_map/while/body/eval_jaxpr/reduce_scatter | solution.py:48
  250.8 1.7 copy.42
  252.6 29.3 %all-gather.2.cloned.1.call-done = f32[36,128,128]{2,1,0:T(8,128)} async-done(((f32[36,16,128]{2,1,0:T(8,128)}), f32[36,128,128]{2,1,0:T(8,128)}) %all-gather.2.cloned.1.call-update) | async-done | bytes 2359312 | tf_op jit(solution)/shard_map/while/body/eval_jaxpr/all_gather | solution.py:49
  281.9 1.9 broadcast_select_fusion.2
  283.8 3.3 fusion.31
  288.8 3.5 constant_dynamic-slice_fusion.8
  292.3 54.6 %all-reduce.8.cloned.1.call-done = (f32[128,128]{1,0:T(8,128)}, f32[18,128,128]{1,2,0:T(8,128)}) async-done(((f32[128,128]{1,0:T(8,128)}, f32[18,128,128]{1,2,0:T(8,128)}), (f32[128,128]{1,0:T(8,128)}, f32[18,128,128]{1,2,0:T(8,128)})) %all-reduce.8.cloned.1.call-update) | async-done | bytes 1245200 | tf_op jit(solution)/shard_map/while/body/eval_jaxpr/psum | solution.py:55
  347.9 3.5 bitcast_dynamic-update-slice_fusion.4
  354.2 27.0 %fusion.30 = f32[36,128,128]{1,2,0:T(8,128)S(1)} fusion(f32[36,18,128,128]{3,2,1,0:T(8,128)} %get-tuple-element.557, bf16[18,6,128,128]{3,2,1,0:T(8,128)(2,1)} %get-tuple-element.586, s32[]{:T(128)S(6)} %select_n.384), kind=kOutput, calls=%fused_computation.6.clone.1 | convolution fusion | flops 16308043776 | bytes 45416452 | tf_op jit(solution)/shard_map/while/body/eval_jaxpr/acxy,cyz->axz/dot_general | solution.py:45
  381.2 2.3 copy.41
  383.6 43.1 %reduce-scatter.2.cloned.1.call-done = f32[36,16,128]{2,0,1:T(8,128)} async-done(((f32[36,128,128]{2,0,1:T(8,128)}), f32[36,16,128]{2,0,1:T(8,128)}) %reduce-scatter.2.cloned.1.call-update) | async-done | bytes 294928 | tf_op jit(solution)/shard_map/while/body/eval_jaxpr/reduce_scatter | solution.py:48
  426.7 1.7 copy.42
  428.6 29.3 %all-gather.2.cloned.1.call-done = f32[36,128,128]{2,1,0:T(8,128)} async-done(((f32[36,16,128]{2,1,0:T(8,128)}), f32[36,128,128]{2,1,0:T(8,128)}) %all-gather.2.cloned.1.call-update) | async-done | bytes 2359312 | tf_op jit(solution)/shard_map/while/body/eval_jaxpr/all_gather | solution.py:49
  457.9 1.9 broadcast_select_fusion.2
  459.8 3.3 fusion.31
  464.8 3.5 constant_dynamic-slice_fusion.8
  468.3 54.6 %all-reduce.8.cloned.1.call-done = (f32[128,128]{1,0:T(8,128)}, f32[18,128,128]{1,2,0:T(8,128)}) async-done(((f32[128,128]{1,0:T(8,128)}, f32[18,128,128]{1,2,0:T(8,128)}), (f32[128,128]{1,0:T(8,128)}, f32[18,128,128]{1,2,0:T(8,128)})) %all-reduce.8.cloned.1.call-update) | async-done | bytes 1245200 | tf_op jit(solution)/shard_map/while/body/eval_jaxpr/psum | solution.py:55
  523.9 3.5 bitcast_dynamic-update-slice_fusion.4
  530.2 27.1 %fusion.30 = f32[36,128,128]{1,2,0:T(8,128)S(1)} fusion(f32[36,18,128,128]{3,2,1,0:T(8,128)} %get-tuple-element.557, bf16[18,6,128,128]{3,2,1,0:T(8,128)(2,1)} %get-tuple-element.586, s32[]{:T(128)S(6)} %select_n.384), kind=kOutput, calls=%fused_computation.6.clone.1 | convolution fusion | flops 16308043776 | bytes 45416452 | tf_op jit(solution)/shard_map/while/body/eval_jaxpr/acxy,cyz->axz/dot_general | solution.py:45
  557.3 2.3 copy.41
  559.6 43.1 %reduce-scatter.2.cloned.1.call-done = f32[36,16,128]{2,0,1:T(8,128)} async-done(((f32[36,128,128]{2,0,1:T(8,128)}), f32[36,16,128]{2,0,1:T(8,128)}) %reduce-scatter.2.cloned.1.call-update) | async-done | bytes 294928 | tf_op jit(solution)/shard_map/while/body/eval_jaxpr/reduce_scatter | solution.py:48
  604.6 29.3 %all-gather.2.cloned.1.call-done = f32[36,128,128]{2,1,0:T(8,128)} async-done(((f32[36,16,128]{2,1,0:T(8,128)}), f32[36,128,128]{2,1,0:T(8,128)}) %all-gather.2.cloned.1.call-update) | async-done | bytes 2359312 | tf_op jit(solution)/shard_map/while/body/eval_jaxpr/all_gather | solution.py:49
  633.9 1.9 broadcast_select_fusion.2
  635.8 3.3 fusion.31
  640.8 3.5 constant_dynamic-slice_fusion.8
  644.3 54.6 %all-reduce.8.cloned.1.call-done = (f32[128,128]{1,0:T(8,128)}, f32[18,128,128]{1,2,0:T(8,128)}) async-done(((f32[128,128]{1,0:T(8,128)}, f32[18,128,128]{1,2,0:T(8,128)}), (f32[128,128]{1,0:T(8,128)}, f32[18,128,128]{1,2,0:T(8,128)})) %all-reduce.8.cloned.1.call-update) | async-done | bytes 1245200 | tf_op jit(solution)/shard_map/while/body/eval_jaxpr/psum | solution.py:55
  699.9 3.5 bitcast_dynamic-update-slice_fusion.4
  706.2 27.0 %fusion.30 = f32[36,128,128]{1,2,0:T(8,128)S(1)} fusion(f32[36,18,128,128]{3,2,1,0:T(8,128)} %get-tuple-element.557, bf16[18,6,128,128]{3,2,1,0:T(8,128)(2,1)} %get-tuple-element.586, s32[]{:T(128)S(6)} %select_n.384), kind=kOutput, calls=%fused_computation.6.clone.1 | convolution fusion | flops 16308043776 | bytes 45416452 | tf_op jit(solution)/shard_map/while/body/eval_jaxpr/acxy,cyz->axz/dot_general | solution.py:45
  733.2 2.3 copy.41
  735.6 43.1 %reduce-scatter.2.cloned.1.call-done = f32[36,16,128]{2,0,1:T(8,128)} async-done(((f32[36,128,128]{2,0,1:T(8,128)}), f32[36,16,128]{2,0,1:T(8,128)}) %reduce-scatter.2.cloned.1.call-update) | async-done | bytes 294928 | tf_op jit(solution)/shard_map/while/body/eval_jaxpr/reduce_scatter | solution.py:48
  778.7 1.7 copy.42
  780.6 29.3 %all-gather.2.cloned.1.call-done = f32[36,128,128]{2,1,0:T(8,128)} async-done(((f32[36,16,128]{2,1,0:T(8,128)}), f32[36,128,128]{2,1,0:T(8,128)}) %all-gather.2.cloned.1.call-update) | async-done | bytes 2359312 | tf_op jit(solution)/shard_map/while/body/eval_jaxpr/all_gather | solution.py:49
  809.9 1.9 broadcast_select_fusion.2
  811.8 3.3 fusion.31
  816.8 3.5 constant_dynamic-slice_fusion.8
  820.2 54.6 %all-reduce.8.cloned.1.call-done = (f32[128,128]{1,0:T(8,128)}, f32[18,128,128]{1,2,0:T(8,128)}) async-done(((f32[128,128]{1,0:T(8,128)}, f32[18,128,128]{1,2,0:T(8,128)}), (f32[128,128]{1,0:T(8,128)}, f32[18,128,128]{1,2,0:T(8,128)})) %all-reduce.8.cloned.1.call-update) | async-done | bytes 1245200 | tf_op jit(solution)/shard_map/while/body/eval_jaxpr/psum | solution.py:55
  875.9 3.5 bitcast_dynamic-update-slice_fusion.4
  882.2 27.0 %fusion.30 = f32[36,128,128]{1,2,0:T(8,128)S(1)} fusion(f32[36,18,128,128]{3,2,1,0:T(8,128)} %get-tuple-element.557, bf16[18,6,128,128]{3,2,1,0:T(8,128)(2,1)} %get-tuple-element.586, s32[]{:T(128)S(6)} %select_n.384), kind=kOutput, calls=%fused_computation.6.clone.1 | convolution fusion | flops 16308043776 | bytes 45416452 | tf_op jit(solution)/shard_map/while/body/eval_jaxpr/acxy,cyz->axz/dot_general | solution.py:45
  909.2 2.3 copy.41
  911.6 43.1 %reduce-scatter.2.cloned.1.call-done = f32[36,16,128]{2,0,1:T(8,128)} async-done(((f32[36,128,128]{2,0,1:T(8,128)}), f32[36,16,128]{2,0,1:T(8,128)}) %reduce-scatter.2.cloned.1.call-update) | async-done | bytes 294928 | tf_op jit(solution)/shard_map/while/body/eval_jaxpr/reduce_scatter | solution.py:48
  954.7 1.7 copy.42
  956.5 29.3 %all-gather.2.cloned.1.call-done = f32[36,128,128]{2,1,0:T(8,128)} async-done(((f32[36,16,128]{2,1,0:T(8,128)}), f32[36,128,128]{2,1,0:T(8,128)}) %all-gather.2.cloned.1.call-update) | async-done | bytes 2359312 | tf_op jit(solution)/shard_map/while/body/eval_jaxpr/all_gather | solution.py:49
  985.9 1.9 broadcast_select_fusion.2
  987.8 3.3 fusion.31
  992.8 3.5 constant_dynamic-slice_fusion.8
  996.2 54.6 %all-reduce.8.cloned.1.call-done = (f32[128,128]{1,0:T(8,128)}, f32[18,128,128]{1,2,0:T(8,128)}) async-done(((f32[128,128]{1,0:T(8,128)}, f32[18,128,128]{1,2,0:T(8,128)}), (f32[128,128]{1,0:T(8,128)}, f32[18,128,128]{1,2,0:T(8,128)})) %all-reduce.8.cloned.1.call-update) | async-done | bytes 1245200 | tf_op jit(solution)/shard_map/while/body/eval_jaxpr/psum | solution.py:55
  1051.8 3.5 bitcast_dynamic-update-slice_fusion.4
  1058.2 27.0 %fusion.30 = f32[36,128,128]{1,2,0:T(8,128)S(1)} fusion(f32[36,18,128,128]{3,2,1,0:T(8,128)} %get-tuple-element.557, bf16[18,6,128,128]{3,2,1,0:T(8,128)(2,1)} %get-tuple-element.586, s32[]{:T(128)S(6)} %select_n.384), kind=kOutput, calls=%fused_computation.6.clone.1 | convolution fusion | flops 16308043776 | bytes 45416452 | tf_op jit(solution)/shard_map/while/body/eval_jaxpr/acxy,cyz->axz/dot_general | solution.py:45
  1085.2 2.3 copy.41
  1087.5 43.1 %reduce-scatter.2.cloned.1.call-done = f32[36,16,128]{2,0,1:T(8,128)} async-done(((f32[36,128,128]{2,0,1:T(8,128)}), f32[36,16,128]{2,0,1:T(8,128)}) %reduce-scatter.2.cloned.1.call-update) | async-done | bytes 294928 | tf_op jit(solution)/shard_map/while/body/eval_jaxpr/reduce_scatter | solution.py:48
  1132.5 29.3 %all-gather.2.cloned.1.call-done = f32[36,128,128]{2,1,0:T(8,128)} async-done(((f32[36,16,128]{2,1,0:T(8,128)}), f32[36,128,128]{2,1,0:T(8,128)}) %all-gather.2.cloned.1.call-update) | async-done | bytes 2359312 | tf_op jit(solution)/shard_map/while/body/eval_jaxpr/all_gather | solution.py:49
  1161.8 1.9 broadcast_select_fusion.2
  1163.7 3.3 fusion.31
  1168.7 3.5 constant_dynamic-slice_fusion.8
  1172.2 54.6 %all-reduce.8.cloned.1.call-done = (f32[128,128]{1,0:T(8,128)}, f32[18,128,128]{1,2,0:T(8,128)}) async-done(((f32[128,128]{1,0:T(8,128)}, f32[18,128,128]{1,2,0:T(8,128)}), (f32[128,128]{1,0:T(8,128)}, f32[18,128,128]{1,2,0:T(8,128)})) %all-reduce.8.cloned.1.call-update) | async-done | bytes 1245200 | tf_op jit(solution)/shard_map/while/body/eval_jaxpr/psum | solution.py:55
  1227.8 3.5 bitcast_dynamic-update-slice_fusion.4
  (136 shorter events, 38.4 us)
Async XLA Ops:
  6.5 30.6 %copy-start = (s32[144,144]{1,0:T(8,128)S(1)}, s32[144,144]{1,0:T(8,128)}, u32[]{:S(2)}) copy-start(s32[144,144]{1,0:T(8,128)} %param.9) | copy-start | bytes 248836
  6.5 172.2 %all-reduce.6.cloned.1.call-start = ((), (), s32[]{:S(2)}) async-start(), calls=%async_computation.1 | async-start | bytes 7077888 | tf_op jit(solution)/shard_map/psum | solution.py:9
  178.7 72.0 %reduce-scatter.2.cloned.1.call-start = ((), (), s32[]{:S(2)}) async-start(), calls=%async_computation.2 | async-start | bytes 2949120 | tf_op jit(solution)/shard_map/while/body/eval_jaxpr/reduce_scatter | solution.py:48
  208.1 73.9 %all-gather.2.cloned.1.call-start = ((), (), s32[]{:S(2)}) async-start(), calls=%async_computation.3 | async-start | bytes 2654208 | tf_op jit(solution)/shard_map/while/body/eval_jaxpr/all_gather | solution.py:49
  252.5 94.4 %all-reduce.8.cloned.1.call-start = ((), (), s32[]{:S(2)}) async-start(), calls=%async_computation.4 | async-start | bytes 2490368 | tf_op jit(solution)/shard_map/while/body/eval_jaxpr/psum | solution.py:55
  288.8 59.1 %copy-start.2 = (f32[36,128,128]{2,1,0:T(8,128)S(1)}, f32[36,128,128]{2,1,0:T(8,128)}, u32[]{:S(2)}) copy-start(f32[36,128,128]{2,1,0:T(8,128)} %all-gather.2.cloned.1.call-done) | copy-start | bytes 7077892 | tf_op jit(solution)/shard_map/while
  351.4 1.6 copy-start.3
  354.2 72.5 %reduce-scatter.2.cloned.1.call-start = ((), (), s32[]{:S(2)}) async-start(), calls=%async_computation.2 | async-start | bytes 2949120 | tf_op jit(solution)/shard_map/while/body/eval_jaxpr/reduce_scatter | solution.py:48
  383.6 74.3 %all-gather.2.cloned.1.call-start = ((), (), s32[]{:S(2)}) async-start(), calls=%async_computation.3 | async-start | bytes 2654208 | tf_op jit(solution)/shard_map/while/body/eval_jaxpr/all_gather | solution.py:49
  428.5 94.4 %all-reduce.8.cloned.1.call-start = ((), (), s32[]{:S(2)}) async-start(), calls=%async_computation.4 | async-start | bytes 2490368 | tf_op jit(solution)/shard_map/while/body/eval_jaxpr/psum | solution.py:55
  464.8 59.1 %copy-start.2 = (f32[36,128,128]{2,1,0:T(8,128)S(1)}, f32[36,128,128]{2,1,0:T(8,128)}, u32[]{:S(2)}) copy-start(f32[36,128,128]{2,1,0:T(8,128)} %all-gather.2.cloned.1.call-done) | copy-start | bytes 7077892 | tf_op jit(solution)/shard_map/while
  527.4 1.6 copy-start.3
  530.2 72.5 %reduce-scatter.2.cloned.1.call-start = ((), (), s32[]{:S(2)}) async-start(), calls=%async_computation.2 | async-start | bytes 2949120 | tf_op jit(solution)/shard_map/while/body/eval_jaxpr/reduce_scatter | solution.py:48
  559.6 74.3 %all-gather.2.cloned.1.call-start = ((), (), s32[]{:S(2)}) async-start(), calls=%async_computation.3 | async-start | bytes 2654208 | tf_op jit(solution)/shard_map/while/body/eval_jaxpr/all_gather | solution.py:49
  604.5 94.4 %all-reduce.8.cloned.1.call-start = ((), (), s32[]{:S(2)}) async-start(), calls=%async_computation.4 | async-start | bytes 2490368 | tf_op jit(solution)/shard_map/while/body/eval_jaxpr/psum | solution.py:55
  640.8 59.1 %copy-start.2 = (f32[36,128,128]{2,1,0:T(8,128)S(1)}, f32[36,128,128]{2,1,0:T(8,128)}, u32[]{:S(2)}) copy-start(f32[36,128,128]{2,1,0:T(8,128)} %all-gather.2.cloned.1.call-done) | copy-start | bytes 7077892 | tf_op jit(solution)/shard_map/while
  703.4 1.6 copy-start.3
  706.2 72.5 %reduce-scatter.2.cloned.1.call-start = ((), (), s32[]{:S(2)}) async-start(), calls=%async_computation.2 | async-start | bytes 2949120 | tf_op jit(solution)/shard_map/while/body/eval_jaxpr/reduce_scatter | solution.py:48
  735.6 74.3 %all-gather.2.cloned.1.call-start = ((), (), s32[]{:S(2)}) async-start(), calls=%async_computation.3 | async-start | bytes 2654208 | tf_op jit(solution)/shard_map/while/body/eval_jaxpr/all_gather | solution.py:49
  780.5 94.4 %all-reduce.8.cloned.1.call-start = ((), (), s32[]{:S(2)}) async-start(), calls=%async_computation.4 | async-start | bytes 2490368 | tf_op jit(solution)/shard_map/while/body/eval_jaxpr/psum | solution.py:55
  816.8 59.1 %copy-start.2 = (f32[36,128,128]{2,1,0:T(8,128)S(1)}, f32[36,128,128]{2,1,0:T(8,128)}, u32[]{:S(2)}) copy-start(f32[36,128,128]{2,1,0:T(8,128)} %all-gather.2.cloned.1.call-done) | copy-start | bytes 7077892 | tf_op jit(solution)/shard_map/while
  879.4 1.6 copy-start.3
  882.2 72.5 %reduce-scatter.2.cloned.1.call-start = ((), (), s32[]{:S(2)}) async-start(), calls=%async_computation.2 | async-start | bytes 2949120 | tf_op jit(solution)/shard_map/while/body/eval_jaxpr/reduce_scatter | solution.py:48
  911.5 74.3 %all-gather.2.cloned.1.call-start = ((), (), s32[]{:S(2)}) async-start(), calls=%async_computation.3 | async-start | bytes 2654208 | tf_op jit(solution)/shard_map/while/body/eval_jaxpr/all_gather | solution.py:49
  956.5 94.4 %all-reduce.8.cloned.1.call-start = ((), (), s32[]{:S(2)}) async-start(), calls=%async_computation.4 | async-start | bytes 2490368 | tf_op jit(solution)/shard_map/while/body/eval_jaxpr/psum | solution.py:55
  992.7 59.1 %copy-start.2 = (f32[36,128,128]{2,1,0:T(8,128)S(1)}, f32[36,128,128]{2,1,0:T(8,128)}, u32[]{:S(2)}) copy-start(f32[36,128,128]{2,1,0:T(8,128)} %all-gather.2.cloned.1.call-done) | copy-start | bytes 7077892 | tf_op jit(solution)/shard_map/while
  1055.3 1.6 copy-start.3
  1058.2 72.5 %reduce-scatter.2.cloned.1.call-start = ((), (), s32[]{:S(2)}) async-start(), calls=%async_computation.2 | async-start | bytes 2949120 | tf_op jit(solution)/shard_map/while/body/eval_jaxpr/reduce_scatter | solution.py:48
  1087.5 74.3 %all-gather.2.cloned.1.call-start = ((), (), s32[]{:S(2)}) async-start(), calls=%async_computation.3 | async-start | bytes 2654208 | tf_op jit(solution)/shard_map/while/body/eval_jaxpr/all_gather | solution.py:49
  1132.4 94.4 %all-reduce.8.cloned.1.call-start = ((), (), s32[]{:S(2)}) async-start(), calls=%async_computation.4 | async-start | bytes 2490368 | tf_op jit(solution)/shard_map/while/body/eval_jaxpr/psum | solution.py:55
  1168.7 59.1 %copy-start.2 = (f32[36,128,128]{2,1,0:T(8,128)S(1)}, f32[36,128,128]{2,1,0:T(8,128)}, u32[]{:S(2)}) copy-start(f32[36,128,128]{2,1,0:T(8,128)} %all-gather.2.cloned.1.call-done) | copy-start | bytes 7077892 | tf_op jit(solution)/shard_map/while
  1231.3 1.6 copy-start.3
  1234.1 0.9 copy-start.1
Sparse Core Ops, SparseCore 0:
  42.2 136.4 all-reduce.5
  208.2 42.5 reduce-scatter.1
  252.6 29.2 all-gather.1
  288.8 58.0 all-reduce.7
  383.7 42.9 reduce-scatter.1
  428.6 29.2 all-gather.1
  464.8 58.0 all-reduce.7
  559.7 42.9 reduce-scatter.1
  604.6 29.2 all-gather.1
  640.8 58.0 all-reduce.7
  735.7 42.9 reduce-scatter.1
  780.6 29.2 all-gather.1
  816.8 58.0 all-reduce.7
  911.6 42.9 reduce-scatter.1
  956.6 29.2 all-gather.1
  992.8 58.0 all-reduce.7
  1087.6 42.9 reduce-scatter.1
  1132.5 29.2 all-gather.1
  1168.7 58.0 all-reduce.7
where the time goes:
time: 1240 us
  waiting for transfers between devices  882 us (71%)
  matrix products  182 us (15%)
  local copies, waits for them, and re-layouts  101 us (8%)
  other arithmetic  62.3 us (5%)
  between operations  13.1 us (1%)
    psum x6, waiting for transfers between devices, advance(): diag_total = lax.psum(diag_term, 'prow')  328 us
    reduce_scatter x6, waiting for transfers between devices, advance(): lax.psum_scatter(partial_value, 'pcol', scatter_dimension=1, tiled=True)  258 us
    all_gather x6, waiting for transfers between devices, advance(): col_whole = lax.all_gather(col_piece, 'pcol', axis=1, tiled=True)  176 us
    dot_general x6, matrix products, advance(): jnp.einsum('acxy,cyz->axz', matrix, other_rows.astype(jnp.float32), preci...  162 us
    psum x1, waiting for transfers between devices, spread(): return lax.psum(kept, axis)  120 us
    unnamed x7, local copies, waits for them, and re-layouts  41.9 us
  transfers between devices with their start and end apart: 19, of which 19 were waited for; matrix products, arithmetic and copies ran while one was open for 3% of the time, Pallas kernels for 0%

commit v1 on v0

--- a/solution.py
+++ b/solution.py
@@ -52,7 +52,7 @@
         diag_term = jnp.einsum(
             "axy,axz->yz", own_col.astype(jnp.float32), inverse_col, precision=lax.Precision.HIGHEST
         )
-        diag_total = lax.psum(diag_term, "prow")
+        diag_total = jnp.sum(lax.all_gather(diag_term, "prow"), axis=0)
         diag_block = lax.dynamic_index_in_dim(dinv, column, 0, keepdims=False) - diag_total
         new_col = jnp.where((row_ids == column)[:, None, None], diag_block[None], inverse_col)
         col_slot = column // col_count

time: 1240 us -> 1230 us (level)
  waiting for transfers between devices: 882 us -> 739 us
  blocking collectives: 0 us -> 95.7 us
  other arithmetic: 62.3 us -> 82 us
  local copies, waits for them, and re-layouts: 101 us -> 118 us
    psum x6 -> x0, waiting for transfers between devices: 328 us -> none  [advance(): diag_total = lax.psum(diag_term, 'prow')]
    psum x1 -> x7, waiting for transfers between devices: 120 us -> 325 us  [spread(): return lax.psum(kept, axis)]
    all_gather x0 -> x6, blocking collectives: none -> 95.7 us  [advance(): diag_total = jnp.sum(lax.all_gather(diag_term, 'prow'), axis=0)]
    all_gather x6, waiting for transfers between devices: 176 us -> 155 us  [advance(): col_whole = lax.all_gather(col_piece, 'pcol', axis=1, tiled=True)]
    while x30 -> x6, local copies, waits for them, and re-layouts: 3.15 us -> 16 us
  transfers between devices with their start and end apart: 19 -> 19, of which waited for: 19 -> 19; matrix products, arithmetic and copies ran while one was open for 3% -> 8% of each run, Pallas kernels for 0% -> 0%
where the time goes in v1:
time: 1230 us
  waiting for transfers between devices  739 us (60%)
  matrix products  178 us (14%)
  local copies, waits for them, and re-layouts  118 us (10%)
  blocking collectives  95.7 us (8%)
  other arithmetic  82 us (7%)
  between operations  13.1 us (1%)
    psum x7, waiting for transfers between devices, spread(): return lax.psum(kept, axis)  325 us
    reduce_scatter x6, waiting for transfers between devices, advance(): lax.psum_scatter(partial_value, 'pcol', scatter_dimension=1, tiled=True)  258 us
    dot_general x6, matrix products, advance(): jnp.einsum('acxy,cyz->axz', matrix, other_rows.astype(jnp.float32), preci...  162 us
    all_gather x6, waiting for transfers between devices, advance(): col_whole = lax.all_gather(col_piece, 'pcol', axis=1, tiled=True)  155 us
    all_gather x6, blocking collectives, advance(): diag_total = jnp.sum(lax.all_gather(diag_term, 'prow'), axis=0)  95.7 us
    unnamed x7, local copies, waits for them, and re-layouts  42 us
    dynamic_update_slice x6, other arithmetic, advance(): lax.dynamic_update_index_in_dim(matrix, jnp.where(pcol_id == column % col...  25.3 us
  transfers between devices with their start and end apart: 19, of which 19 were waited for; matrix products, arithmetic and copies ran while one was open for 8% of the time, Pallas kernels for 0%

profile of v1, /device:TPU:0, one launch (start us, length us, event | category | flops | bytes accessed | tf_op | source)
XLA Modules:
  0.0 1226.8 jit_solution(9912525630681480986)
XLA Ops:
  6.5 30.5 %copy.54 = f32[36,1,18,1,128,128]{5,4,3,2,1,0:T(8,128)} copy(f32[36,1,18,1,128,128]{5,4,3,2,1,0:T(8,128)} %param.6) | data formatting | bytes 84934656
  37.8 4.3 fusion.17
  42.3 10.4 copy.29
  52.7 6.5 bitcast_select_fusion.2
  59.2 119.5 %all-reduce.3.cloned.1.call-done = bf16[18,6,128,128]{3,2,1,0:T(8,128)(2,1)} async-done(((bf16[18,6,128,128]{3,2,1,0:T(8,128)(2,1)}), bf16[18,6,128,128]{3,2,1,0:T(8,128)(2,1)}) %all-reduce.3.cloned.1.call-update) | async-done | bytes 3538960 | tf_op jit(solution)/shard_map/psum | solution.py:9
  178.7 1040.6 %while.18 = (s32[]{:T(128)}, f32[36,18,128,128]{3,2,1,0:T(8,128)}, s32[]{:T(128)}, f32[6,128,128]{2,1,0:T(8,128)}, bf16[36,6,128,128]{2,3,0,1:T(8,128)(2,1)}, /*...) while((s32[]{:T(128)}, f32[36,18,128,128]{3,2,1,0:T(8,128)}, ...), condition=%wide.region_5.6_spmd.clone.clone, body=%wide.region_1.5_spmd.clone.clone.sunk | while | flops 17217617920 | bytes 108233968 | solution.py:76
  178.7 27.0 %fusion.32 = f32[36,128,128]{1,2,0:T(8,128)S(1)} fusion(f32[36,18,128,128]{3,2,1,0:T(8,128)} %get-tuple-element.552, bf16[18,6,128,128]{3,2,1,0:T(8,128)(2,1)} %get-tuple-element.582, s32[]{:T(128)S(6)} %select_n.384), kind=kOutput, calls=%fused_computation.6.clone.1 | convolution fusion | flops 16308043776 | bytes 45416452 | tf_op jit(solution)/shard_map/while/body/eval_jaxpr/acxy,cyz->axz/dot_general | solution.py:45
  208.0 42.6 %reduce-scatter.2.cloned.1.call-done = f32[36,16,128]{2,0,1:T(8,128)} async-done(((f32[36,128,128]{2,0,1:T(8,128)}), f32[36,16,128]{2,0,1:T(8,128)}) %reduce-scatter.2.cloned.1.call-update) | async-done | bytes 294928 | tf_op jit(solution)/shard_map/while/body/eval_jaxpr/reduce_scatter | solution.py:48
  252.6 3.3 constant_dynamic-slice_fusion.8
  255.9 25.9 %all-gather.7.cloned.1.call-done = f32[36,128,128]{2,1,0:T(8,128)} async-done(((f32[36,16,128]{2,1,0:T(8,128)}), f32[36,128,128]{2,1,0:T(8,128)}) %all-gather.7.cloned.1.call-update) | async-done | bytes 2359312 | tf_op jit(solution)/shard_map/while/body/eval_jaxpr/all_gather | solution.py:49
  284.8 2.7 copy.41
  289.9 2.7 fusion.33
  292.6 16.0 %all-gather.4 = f32[512,128]{1,0:T(8,128)S(1)} all-gather(f32[128,128]{1,0:T(8,128)S(1)} %fusion.33), channel_id=2, replica_groups=mesh['prow'=4,'pcol'=8] {'prow'}, dimensions={0}, use_global_device_ids=true | all-gather | bytes 327680 | tf_op jit(solution)/shard_map/while/body/eval_jaxpr/all_gather | solution.py:55
  309.5 4.2 bitcast_dynamic-update-slice_fusion.4
  315.1 34.2 %all-reduce.5.cloned.1.call-done = f32[18,128,128]{1,2,0:T(8,128)} async-done(((f32[18,128,128]{1,2,0:T(8,128)}), f32[18,128,128]{1,2,0:T(8,128)}) %all-reduce.5.cloned.1.call-update) | async-done | bytes 1179664 | tf_op jit(solution)/shard_map/while/body/eval_jaxpr/psum | solution.py:9
  349.3 2.5 bitcast_dynamic-update-slice_fusion.5
  351.8 27.0 %fusion.32 = f32[36,128,128]{1,2,0:T(8,128)S(1)} fusion(f32[36,18,128,128]{3,2,1,0:T(8,128)} %get-tuple-element.552, bf16[18,6,128,128]{3,2,1,0:T(8,128)(2,1)} %get-tuple-element.582, s32[]{:T(128)S(6)} %select_n.384), kind=kOutput, calls=%fused_computation.6.clone.1 | convolution fusion | flops 16308043776 | bytes 45416452 | tf_op jit(solution)/shard_map/while/body/eval_jaxpr/acxy,cyz->axz/dot_general | solution.py:45
  381.0 43.0 %reduce-scatter.2.cloned.1.call-done = f32[36,16,128]{2,0,1:T(8,128)} async-done(((f32[36,128,128]{2,0,1:T(8,128)}), f32[36,16,128]{2,0,1:T(8,128)}) %reduce-scatter.2.cloned.1.call-update) | async-done | bytes 294928 | tf_op jit(solution)/shard_map/while/body/eval_jaxpr/reduce_scatter | solution.py:48
  426.0 3.3 constant_dynamic-slice_fusion.8
  429.4 25.9 %all-gather.7.cloned.1.call-done = f32[36,128,128]{2,1,0:T(8,128)} async-done(((f32[36,16,128]{2,1,0:T(8,128)}), f32[36,128,128]{2,1,0:T(8,128)}) %all-gather.7.cloned.1.call-update) | async-done | bytes 2359312 | tf_op jit(solution)/shard_map/while/body/eval_jaxpr/all_gather | solution.py:49
  458.3 2.7 copy.41
  463.4 2.7 fusion.33
  466.1 16.0 %all-gather.4 = f32[512,128]{1,0:T(8,128)S(1)} all-gather(f32[128,128]{1,0:T(8,128)S(1)} %fusion.33), channel_id=2, replica_groups=mesh['prow'=4,'pcol'=8] {'prow'}, dimensions={0}, use_global_device_ids=true | all-gather | bytes 327680 | tf_op jit(solution)/shard_map/while/body/eval_jaxpr/all_gather | solution.py:55
  483.0 4.2 bitcast_dynamic-update-slice_fusion.4
  488.6 34.2 %all-reduce.5.cloned.1.call-done = f32[18,128,128]{1,2,0:T(8,128)} async-done(((f32[18,128,128]{1,2,0:T(8,128)}), f32[18,128,128]{1,2,0:T(8,128)}) %all-reduce.5.cloned.1.call-update) | async-done | bytes 1179664 | tf_op jit(solution)/shard_map/while/body/eval_jaxpr/psum | solution.py:9
  522.8 2.5 bitcast_dynamic-update-slice_fusion.5
  525.3 27.0 %fusion.32 = f32[36,128,128]{1,2,0:T(8,128)S(1)} fusion(f32[36,18,128,128]{3,2,1,0:T(8,128)} %get-tuple-element.552, bf16[18,6,128,128]{3,2,1,0:T(8,128)(2,1)} %get-tuple-element.582, s32[]{:T(128)S(6)} %select_n.384), kind=kOutput, calls=%fused_computation.6.clone.1 | convolution fusion | flops 16308043776 | bytes 45416452 | tf_op jit(solution)/shard_map/while/body/eval_jaxpr/acxy,cyz->axz/dot_general | solution.py:45
  554.6 43.0 %reduce-scatter.2.cloned.1.call-done = f32[36,16,128]{2,0,1:T(8,128)} async-done(((f32[36,128,128]{2,0,1:T(8,128)}), f32[36,16,128]{2,0,1:T(8,128)}) %reduce-scatter.2.cloned.1.call-update) | async-done | bytes 294928 | tf_op jit(solution)/shard_map/while/body/eval_jaxpr/reduce_scatter | solution.py:48
  599.6 3.3 constant_dynamic-slice_fusion.8
  602.9 25.9 %all-gather.7.cloned.1.call-done = f32[36,128,128]{2,1,0:T(8,128)} async-done(((f32[36,16,128]{2,1,0:T(8,128)}), f32[36,128,128]{2,1,0:T(8,128)}) %all-gather.7.cloned.1.call-update) | async-done | bytes 2359312 | tf_op jit(solution)/shard_map/while/body/eval_jaxpr/all_gather | solution.py:49
  631.8 2.7 copy.41
  636.9 2.7 fusion.33
  639.6 16.0 %all-gather.4 = f32[512,128]{1,0:T(8,128)S(1)} all-gather(f32[128,128]{1,0:T(8,128)S(1)} %fusion.33), channel_id=2, replica_groups=mesh['prow'=4,'pcol'=8] {'prow'}, dimensions={0}, use_global_device_ids=true | all-gather | bytes 327680 | tf_op jit(solution)/shard_map/while/body/eval_jaxpr/all_gather | solution.py:55
  656.5 4.2 bitcast_dynamic-update-slice_fusion.4
  662.1 34.2 %all-reduce.5.cloned.1.call-done = f32[18,128,128]{1,2,0:T(8,128)} async-done(((f32[18,128,128]{1,2,0:T(8,128)}), f32[18,128,128]{1,2,0:T(8,128)}) %all-reduce.5.cloned.1.call-update) | async-done | bytes 1179664 | tf_op jit(solution)/shard_map/while/body/eval_jaxpr/psum | solution.py:9
  696.3 2.5 bitcast_dynamic-update-slice_fusion.5
  698.8 27.0 %fusion.32 = f32[36,128,128]{1,2,0:T(8,128)S(1)} fusion(f32[36,18,128,128]{3,2,1,0:T(8,128)} %get-tuple-element.552, bf16[18,6,128,128]{3,2,1,0:T(8,128)(2,1)} %get-tuple-element.582, s32[]{:T(128)S(6)} %select_n.384), kind=kOutput, calls=%fused_computation.6.clone.1 | convolution fusion | flops 16308043776 | bytes 45416452 | tf_op jit(solution)/shard_map/while/body/eval_jaxpr/acxy,cyz->axz/dot_general | solution.py:45
  728.1 43.0 %reduce-scatter.2.cloned.1.call-done = f32[36,16,128]{2,0,1:T(8,128)} async-done(((f32[36,128,128]{2,0,1:T(8,128)}), f32[36,16,128]{2,0,1:T(8,128)}) %reduce-scatter.2.cloned.1.call-update) | async-done | bytes 294928 | tf_op jit(solution)/shard_map/while/body/eval_jaxpr/reduce_scatter | solution.py:48
  773.1 3.3 constant_dynamic-slice_fusion.8
  776.4 25.9 %all-gather.7.cloned.1.call-done = f32[36,128,128]{2,1,0:T(8,128)} async-done(((f32[36,16,128]{2,1,0:T(8,128)}), f32[36,128,128]{2,1,0:T(8,128)}) %all-gather.7.cloned.1.call-update) | async-done | bytes 2359312 | tf_op jit(solution)/shard_map/while/body/eval_jaxpr/all_gather | solution.py:49
  805.3 2.7 copy.41
  810.4 2.7 fusion.33
  813.1 16.0 %all-gather.4 = f32[512,128]{1,0:T(8,128)S(1)} all-gather(f32[128,128]{1,0:T(8,128)S(1)} %fusion.33), channel_id=2, replica_groups=mesh['prow'=4,'pcol'=8] {'prow'}, dimensions={0}, use_global_device_ids=true | all-gather | bytes 327680 | tf_op jit(solution)/shard_map/while/body/eval_jaxpr/all_gather | solution.py:55
  830.0 4.2 bitcast_dynamic-update-slice_fusion.4
  835.6 34.2 %all-reduce.5.cloned.1.call-done = f32[18,128,128]{1,2,0:T(8,128)} async-done(((f32[18,128,128]{1,2,0:T(8,128)}), f32[18,128,128]{1,2,0:T(8,128)}) %all-reduce.5.cloned.1.call-update) | async-done | bytes 1179664 | tf_op jit(solution)/shard_map/while/body/eval_jaxpr/psum | solution.py:9
  869.8 2.5 bitcast_dynamic-update-slice_fusion.5
  872.3 27.1 %fusion.32 = f32[36,128,128]{1,2,0:T(8,128)S(1)} fusion(f32[36,18,128,128]{3,2,1,0:T(8,128)} %get-tuple-element.552, bf16[18,6,128,128]{3,2,1,0:T(8,128)(2,1)} %get-tuple-element.582, s32[]{:T(128)S(6)} %select_n.384), kind=kOutput, calls=%fused_computation.6.clone.1 | convolution fusion | flops 16308043776 | bytes 45416452 | tf_op jit(solution)/shard_map/while/body/eval_jaxpr/acxy,cyz->axz/dot_general | solution.py:45
  901.6 43.0 %reduce-scatter.2.cloned.1.call-done = f32[36,16,128]{2,0,1:T(8,128)} async-done(((f32[36,128,128]{2,0,1:T(8,128)}), f32[36,16,128]{2,0,1:T(8,128)}) %reduce-scatter.2.cloned.1.call-update) | async-done | bytes 294928 | tf_op jit(solution)/shard_map/while/body/eval_jaxpr/reduce_scatter | solution.py:48
  946.6 3.3 constant_dynamic-slice_fusion.8
  950.0 25.9 %all-gather.7.cloned.1.call-done = f32[36,128,128]{2,1,0:T(8,128)} async-done(((f32[36,16,128]{2,1,0:T(8,128)}), f32[36,128,128]{2,1,0:T(8,128)}) %all-gather.7.cloned.1.call-update) | async-done | bytes 2359312 | tf_op jit(solution)/shard_map/while/body/eval_jaxpr/all_gather | solution.py:49
  978.9 2.7 copy.41
  984.0 2.7 fusion.33
  986.7 16.0 %all-gather.4 = f32[512,128]{1,0:T(8,128)S(1)} all-gather(f32[128,128]{1,0:T(8,128)S(1)} %fusion.33), channel_id=2, replica_groups=mesh['prow'=4,'pcol'=8] {'prow'}, dimensions={0}, use_global_device_ids=true | all-gather | bytes 327680 | tf_op jit(solution)/shard_map/while/body/eval_jaxpr/all_gather | solution.py:55
  1003.6 4.2 bitcast_dynamic-update-slice_fusion.4
  1009.2 34.2 %all-reduce.5.cloned.1.call-done = f32[18,128,128]{1,2,0:T(8,128)} async-done(((f32[18,128,128]{1,2,0:T(8,128)}), f32[18,128,128]{1,2,0:T(8,128)}) %all-reduce.5.cloned.1.call-update) | async-done | bytes 1179664 | tf_op jit(solution)/shard_map/while/body/eval_jaxpr/psum | solution.py:9
  1045.9 27.0 %fusion.32 = f32[36,128,128]{1,2,0:T(8,128)S(1)} fusion(f32[36,18,128,128]{3,2,1,0:T(8,128)} %get-tuple-element.552, bf16[18,6,128,128]{3,2,1,0:T(8,128)(2,1)} %get-tuple-element.582, s32[]{:T(128)S(6)} %select_n.384), kind=kOutput, calls=%fused_computation.6.clone.1 | convolution fusion | flops 16308043776 | bytes 45416452 | tf_op jit(solution)/shard_map/while/body/eval_jaxpr/acxy,cyz->axz/dot_general | solution.py:45
  1075.1 43.0 %reduce-scatter.2.cloned.1.call-done = f32[36,16,128]{2,0,1:T(8,128)} async-done(((f32[36,128,128]{2,0,1:T(8,128)}), f32[36,16,128]{2,0,1:T(8,128)}) %reduce-scatter.2.cloned.1.call-update) | async-done | bytes 294928 | tf_op jit(solution)/shard_map/while/body/eval_jaxpr/reduce_scatter | solution.py:48
  1120.1 3.3 constant_dynamic-slice_fusion.8
  1123.4 25.9 %all-gather.7.cloned.1.call-done = f32[36,128,128]{2,1,0:T(8,128)} async-done(((f32[36,16,128]{2,1,0:T(8,128)}), f32[36,128,128]{2,1,0:T(8,128)}) %all-gather.7.cloned.1.call-update) | async-done | bytes 2359312 | tf_op jit(solution)/shard_map/while/body/eval_jaxpr/all_gather | solution.py:49
  1152.4 2.7 copy.41
  1157.5 2.7 fusion.33
  1160.1 16.0 %all-gather.4 = f32[512,128]{1,0:T(8,128)S(1)} all-gather(f32[128,128]{1,0:T(8,128)S(1)} %fusion.33), channel_id=2, replica_groups=mesh['prow'=4,'pcol'=8] {'prow'}, dimensions={0}, use_global_device_ids=true | all-gather | bytes 327680 | tf_op jit(solution)/shard_map/while/body/eval_jaxpr/all_gather | solution.py:55
  1177.1 4.2 bitcast_dynamic-update-slice_fusion.4
  1182.6 34.2 %all-reduce.5.cloned.1.call-done = f32[18,128,128]{1,2,0:T(8,128)} async-done(((f32[18,128,128]{1,2,0:T(8,128)}), f32[18,128,128]{1,2,0:T(8,128)}) %all-reduce.5.cloned.1.call-update) | async-done | bytes 1179664 | tf_op jit(solution)/shard_map/while/body/eval_jaxpr/psum | solution.py:9
  (124 shorter events, 77.7 us)
Async XLA Ops:
  6.5 30.6 %copy-start = (s32[144,144]{1,0:T(8,128)S(1)}, s32[144,144]{1,0:T(8,128)}, u32[]{:S(2)}) copy-start(s32[144,144]{1,0:T(8,128)} %param.9) | copy-start | bytes 248836
  6.5 172.2 %all-reduce.3.cloned.1.call-start = ((), (), s32[]{:S(2)}) async-start(), calls=%async_computation.1 | async-start | bytes 7077888 | tf_op jit(solution)/shard_map/psum | solution.py:9
  178.7 71.9 %reduce-scatter.2.cloned.1.call-start = ((), (), s32[]{:S(2)}) async-start(), calls=%async_computation.2 | async-start | bytes 2949120 | tf_op jit(solution)/shard_map/while/body/eval_jaxpr/reduce_scatter | solution.py:48
  208.0 73.8 %all-gather.7.cloned.1.call-start = ((), (), s32[]{:S(2)}) async-start(), calls=%async_computation.3 | async-start | bytes 2654208 | tf_op jit(solution)/shard_map/while/body/eval_jaxpr/all_gather | solution.py:49
  252.4 96.9 %all-reduce.5.cloned.1.call-start = ((), (), s32[]{:S(2)}) async-start(), calls=%async_computation.4 | async-start | bytes 2359296 | tf_op jit(solution)/shard_map/while/body/eval_jaxpr/psum | solution.py:9
  351.8 72.3 %reduce-scatter.2.cloned.1.call-start = ((), (), s32[]{:S(2)}) async-start(), calls=%async_computation.2 | async-start | bytes 2949120 | tf_op jit(solution)/shard_map/while/body/eval_jaxpr/reduce_scatter | solution.py:48
  381.0 74.3 %all-gather.7.cloned.1.call-start = ((), (), s32[]{:S(2)}) async-start(), calls=%async_computation.3 | async-start | bytes 2654208 | tf_op jit(solution)/shard_map/while/body/eval_jaxpr/all_gather | solution.py:49
  425.9 96.9 %all-reduce.5.cloned.1.call-start = ((), (), s32[]{:S(2)}) async-start(), calls=%async_computation.4 | async-start | bytes 2359296 | tf_op jit(solution)/shard_map/while/body/eval_jaxpr/psum | solution.py:9
  525.3 72.3 %reduce-scatter.2.cloned.1.call-start = ((), (), s32[]{:S(2)}) async-start(), calls=%async_computation.2 | async-start | bytes 2949120 | tf_op jit(solution)/shard_map/while/body/eval_jaxpr/reduce_scatter | solution.py:48
  554.5 74.3 %all-gather.7.cloned.1.call-start = ((), (), s32[]{:S(2)}) async-start(), calls=%async_computation.3 | async-start | bytes 2654208 | tf_op jit(solution)/shard_map/while/body/eval_jaxpr/all_gather | solution.py:49
  599.4 96.9 %all-reduce.5.cloned.1.call-start = ((), (), s32[]{:S(2)}) async-start(), calls=%async_computation.4 | async-start | bytes 2359296 | tf_op jit(solution)/shard_map/while/body/eval_jaxpr/psum | solution.py:9
  698.8 72.3 %reduce-scatter.2.cloned.1.call-start = ((), (), s32[]{:S(2)}) async-start(), calls=%async_computation.2 | async-start | bytes 2949120 | tf_op jit(solution)/shard_map/while/body/eval_jaxpr/reduce_scatter | solution.py:48
  728.0 74.3 %all-gather.7.cloned.1.call-start = ((), (), s32[]{:S(2)}) async-start(), calls=%async_computation.3 | async-start | bytes 2654208 | tf_op jit(solution)/shard_map/while/body/eval_jaxpr/all_gather | solution.py:49
  772.9 96.9 %all-reduce.5.cloned.1.call-start = ((), (), s32[]{:S(2)}) async-start(), calls=%async_computation.4 | async-start | bytes 2359296 | tf_op jit(solution)/shard_map/while/body/eval_jaxpr/psum | solution.py:9
  872.3 72.4 %reduce-scatter.2.cloned.1.call-start = ((), (), s32[]{:S(2)}) async-start(), calls=%async_computation.2 | async-start | bytes 2949120 | tf_op jit(solution)/shard_map/while/body/eval_jaxpr/reduce_scatter | solution.py:48
  901.6 74.3 %all-gather.7.cloned.1.call-start = ((), (), s32[]{:S(2)}) async-start(), calls=%async_computation.3 | async-start | bytes 2654208 | tf_op jit(solution)/shard_map/while/body/eval_jaxpr/all_gather | solution.py:49
  946.5 96.9 %all-reduce.5.cloned.1.call-start = ((), (), s32[]{:S(2)}) async-start(), calls=%async_computation.4 | async-start | bytes 2359296 | tf_op jit(solution)/shard_map/while/body/eval_jaxpr/psum | solution.py:9
  1045.9 72.3 %reduce-scatter.2.cloned.1.call-start = ((), (), s32[]{:S(2)}) async-start(), calls=%async_computation.2 | async-start | bytes 2949120 | tf_op jit(solution)/shard_map/while/body/eval_jaxpr/reduce_scatter | solution.py:48
  1075.1 74.3 %all-gather.7.cloned.1.call-start = ((), (), s32[]{:S(2)}) async-start(), calls=%async_computation.3 | async-start | bytes 2654208 | tf_op jit(solution)/shard_map/while/body/eval_jaxpr/all_gather | solution.py:49
  1119.9 96.9 %all-reduce.5.cloned.1.call-start = ((), (), s32[]{:S(2)}) async-start(), calls=%async_computation.4 | async-start | bytes 2359296 | tf_op jit(solution)/shard_map/while/body/eval_jaxpr/psum | solution.py:9
  1219.4 0.9 copy-start.1
Sparse Core Ops, SparseCore 0:
  42.2 136.4 all-reduce.2
  208.1 42.4 reduce-scatter.1
  252.5 29.2 all-gather.6
  290.0 59.2 all-reduce.4
  381.1 42.9 reduce-scatter.1
  426.0 29.2 all-gather.6
  463.5 59.2 all-reduce.4
  554.6 42.9 reduce-scatter.1
  599.5 29.2 all-gather.6
  637.0 59.2 all-reduce.4
  728.1 42.9 reduce-scatter.1
  773.0 29.2 all-gather.6
  810.5 59.2 all-reduce.4
  901.7 42.9 reduce-scatter.1
  946.6 29.2 all-gather.6
  984.1 59.2 all-reduce.4
  1075.2 42.9 reduce-scatter.1
  1120.1 29.2 all-gather.6
  1157.6 59.2 all-reduce.4
